TPU v7x, 768 devices: a whole 4x8x12 slice. The times are simulated.
768 devices in a mesh: seq: 32 (over y_hi, x, core), mp: 24 (over z, y_lo).
Axes of the slice: x: 4, y: 8 (y_hi: 4, y_lo: 2; y = y_hi * 2 + y_lo), z: 12, core: 2. Of those that a mesh axis runs over, the one named last changes fastest.
Arguments:
- hidden_in: bfloat16 [16384, 5376], P('seq'), may hold values from -6 to 6
- norm_gain: float32 [5376], replicated, may hold values from 0.5 to 1.5
- query_weight: bfloat16 [5376, 3072], P(None, 'mp'), as said below
- kv_weight: bfloat16 [5376, 6144], P(None, 'mp'), as said below
- out_weight: bfloat16 [3072, 5376], P('mp'), may hold values from -0.875 to 0.875
Outputs:
- attn_out: bfloat16 [5376, 16384], P('mp', 'seq')
Inputs may be any that keep to these rules, and one draw needn't show every extreme that they name: `query_weight`: query projection columns of mean zero scaled by the fan-in. `kv_weight`: key and value projection columns of mean zero; the columns of query heads 2j and 2j+1 are equal, one key-value head shared by the pair.
All inputs are finite; a program needn't handle non-finite values.
Results may differ from a plain program's by a relative error of at most 0.023.
Values may be sent and summed in bfloat16 or wider, within the bound.
A program may use at most 64 MiB of HBM per device.

v0:
```python
import math

import jax
import jax.numpy as jnp
from jax import lax
from jax.sharding import PartitionSpec as P

WINDOW = 1024


def shifted(block, axis, distance):
    devices = range(lax.axis_size(axis))
    route = [(i - distance, i) for i in devices if i - distance in devices]
    return lax.ppermute(block, axis, route)


def rotate_half(tensor, positions):
    half = tensor.shape[-1] // 2
    freq = jnp.exp(
        -math.log(10000.0) * jnp.arange(half, dtype=jnp.float32) * (2.0 / tensor.shape[-1])
    )
    angle = positions[:, None] * freq[None, :]
    cosine = jnp.cos(angle)
    sine = jnp.sin(angle)
    first = tensor[:, :half]
    second = tensor[:, half:]
    return jnp.concatenate(
        [first * cosine - second * sine, second * cosine + first * sine], axis=-1
    )


def per_device(hidden_in, norm_gain, query_weight, kv_weight, out_weight):
    rows = hidden_in.shape[0]
    head_size = query_weight.shape[1]
    widths = hidden_in.astype(jnp.float32)
    inverse = lax.rsqrt(jnp.mean(widths * widths, axis=-1, keepdims=True) + 1e-06)
    normed = (widths * inverse * norm_gain[None, :]).astype(jnp.bfloat16)
    first_pos = lax.axis_index("seq") * rows
    positions = (first_pos + jnp.arange(rows, dtype=jnp.int32)).astype(jnp.float32)
    queries = rotate_half(
        jnp.dot(normed, query_weight, preferred_element_type=jnp.float32), positions
    ).astype(jnp.bfloat16)
    projected = jnp.dot(normed, kv_weight, preferred_element_type=jnp.float32)
    keys = rotate_half(projected[:, :head_size], positions).astype(jnp.bfloat16)
    values = projected[:, head_size:].astype(jnp.bfloat16)
    reach = -(-WINDOW // rows)
    key_parts = []
    value_parts = []
    for distance in range(reach, 0, -1):
        moved_keys, moved_values = shifted((keys, values), "seq", distance)
        key_parts.append(moved_keys)
        value_parts.append(moved_values)
    context_keys = jnp.concatenate(key_parts + [keys], axis=0)
    context_values = jnp.concatenate(value_parts + [values], axis=0)
    context_pos = first_pos - reach * rows + jnp.arange((reach + 1) * rows, dtype=jnp.int32)
    block = min(rows, 512)
    scores = lax.dot_general(
        queries, context_keys, (((1,), (1,)), ((), ())), preferred_element_type=jnp.float32
    )
    scores = scores * (1.0 / math.sqrt(168.0))
    query_pos = first_pos + 0 + jnp.arange(block, dtype=jnp.int32)
    valid = (
        (context_pos[None, :] <= query_pos[:, None])
        & (query_pos[:, None] - context_pos[None, :] < WINDOW)
        & (context_pos[None, :] >= 0)
    )
    scores = jnp.where(valid, scores, jnp.float32(-1e30))
    highest = jnp.max(scores, axis=-1, keepdims=True)
    expo = jnp.exp(scores - highest)
    probs = (expo / jnp.sum(expo, axis=-1, keepdims=True)).astype(jnp.bfloat16)
    outputs = jnp.dot(probs, context_values, preferred_element_type=jnp.float32).astype(
        jnp.bfloat16
    )
    return lax.psum_scatter(
        lax.dot_general(
            out_weight, outputs, (((0,), (1,)), ((), ())), preferred_element_type=jnp.float32
        ).astype(jnp.bfloat16),
        "mp",
        scatter_dimension=0,
        tiled=True,
    )


def solution(mesh):
    in_specs = (P("seq", None), P(), P(None, "mp"), P(None, "mp"), P("mp", None))
    out_specs = P("mp", "seq")
    return jax.shard_map(
        per_device, mesh=mesh, in_specs=in_specs, out_specs=out_specs, check_vma=False
    )
```

profile of v0, /device:TPU:20, one launch (start us, length us, event | category | flops | bytes accessed | tf_op | source)
XLA Modules:
  0.0 209.2 jit_solution(14514630925355426844)
XLA Ops:
  6.5 0.0 copy-start
  6.5 0.0 copy-start.3
  6.5 0.0 reduce-scatter.4.cloned.1.call-start
  6.6 3.9 %fusion = f32[512]{0:T(512)S(1)} fusion(bf16[512,5376]{1,0:T(8,128)(2,1)} %param.5), kind=kLoop, calls=%fused_computation.2 | loop fusion | flops 8257024 | bytes 5507072 | tf_op jit(solution)/shard_map/reduce_sum | solution.py:36
  10.4 0.0 copy-done.3
  10.5 0.0 copy-start.1
  10.5 5.2 %fusion.10 = f32[512,128]{0,1:T(8,128)S(1)} fusion(bf16[5376,128]{1,0:T(8,128)(2,1)} %param.7, bf16[512,5376]{1,0:T(8,128)(2,1)} %param.5, f32[5376]{0:T(1024)S(1)} %copy-done.3, f32[512]{0:T(512)S(1)} %add_rsqrt_fusion), kind=kOutput, calls=%fused_computation.16 | convolution fusion | flops 715653120 | bytes 7166976 | tf_op jit(solution)/shard_map/dot_general | solution.py:41
  15.6 0.0 copy-done
  15.6 0.0 copy-done.1
  15.6 2.0 fusion.8
  17.7 0.6 fusion.40
  18.3 1.9 collective-permute-start.1
  20.2 3.1 %collective-permute-start = (bf16[512,128]{0,1:T(8,128)(2,1)S(1)}, bf16[512,128]{0,1:T(8,128)(2,1)}, u32[]{:S(2)}, u32[]{:S(2)}) collective-permute-start(bf16[512,128]{0,1:T(8,128)(2,1)S(1)} %pad_maximum_fusion), channel_id=1, source_target_pairs={{0,48},{24,72},{48,96},{72,120},{96,144},{120,168},{144,192},{168,... | collective-permute-start | bytes 393224 | tf_op jit(solution)/shard_map/ppermute | solution.py:14
  23.3 5.4 %collective-permute-start.3 = (bf16[512,128]{0,1:T(8,128)(2,1)S(1)}, bf16[512,128]{0,1:T(8,128)(2,1)S(1)}, u32[]{:S(2)}, u32[]{:S(2)}) collective-permute-start(bf16[512,128]{0,1:T(8,128)(2,1)S(1)} %slice.38), channel_id=1, source_target_pairs={{0,24},{24,48},{48,72},{72,96},{96,120},{120,144},{144,168},{168,1... | collective-permute-start | bytes 393224 | tf_op jit(solution)/shard_map/ppermute | solution.py:14
  28.8 3.4 %collective-permute-start.2 = (bf16[512,128]{0,1:T(8,128)(2,1)S(1)}, bf16[512,128]{0,1:T(8,128)(2,1)S(1)}, u32[]{:S(2)}, u32[]{:S(2)}) collective-permute-start(bf16[512,128]{0,1:T(8,128)(2,1)S(1)} %slice.38), channel_id=1, source_target_pairs={{0,48},{24,72},{48,96},{72,120},{96,144},{120,168},{144,192},{168,... | collective-permute-start | bytes 393224 | tf_op jit(solution)/shard_map/ppermute | solution.py:14
  32.2 0.0 collective-permute-done.1
  32.3 0.0 collective-permute-done
  32.3 2.3 %fusion.54 = (f32[512]{0:T(512)S(1)}, f32[512,1536]{1,0:T(8,128)S(1)}) fusion(bf16[512,64]{0,1:T(8,128)(2,1)S(1)} %get-tuple-element.9, bf16[512,64]{0,1:T(8,128)(2,1)S(1)} %get-tuple-element.10, bf16[512,128]{0,1:T(8,128)(2,1)} %collective-permute-done.1, bf16[512,128]{0,1:T(8,128)(2,1)} %collective-permute-done, ...), kind=kOutput, calls=%fused_computation.62 | convolution fusion | flops 209452544 | bytes 3681792 | tf_op jit(solution)/shard_map/dot_general | solution.py:57
  34.6 0.0 copy-start.2
  34.6 1.7 copy-done.2
  36.2 0.6 fusion.7
  36.8 0.0 collective-permute-done.3
  36.8 0.0 collective-permute-done.2
  36.8 7.6 %fusion.3 = bf16[5376,512]{0,1:T(8,128)(2,1)} fusion(bf16[128,5376]{1,0:T(8,128)(2,1)} %param.9, f32[512,1536]{1,0:T(8,128)} %copy-done.2, f32[512]{0:T(512)S(1)} %fusion.7, f32[512]{0:T(512)S(1)} %get-tuple-element.11, bf16[512,128]{0,1:T(8,128)(2,1)S(1)} %slice.38, bf16[512,128]{0,1:T(8,128)(2,1)S(1)} %collective-permute-done.3, ...), kind=kOutput, calls=%fused_computation.6 | convolution fusion | flops 912326656 | bytes 10424320 | tf_op jit(solution)/shard_map/dot_general | solution.py:75
  44.4 8.3 %copy.8 = bf16[5376,512]{1,0:T(8,128)(2,1)} copy(bf16[5376,512]{0,1:T(8,128)(2,1)} %fusion.3) | data formatting | bytes 11010048
  52.7 0.0 reduce-scatter.4.cloned.1.call-update
  52.7 149.6 %reduce-scatter.4.cloned.1.call-done = bf16[224,512]{1,0:T(8,128)(2,1)} async-done(((bf16[5376,512]{1,0:T(8,128)(2,1)}), bf16[224,512]{1,0:T(8,128)(2,1)}) %reduce-scatter.4.cloned.1.call-update) | async-done | bytes 229392 | tf_op jit(solution)/shard_map/reduce_scatter | solution.py:74
  (8 shorter events, 0.1 us)
Async XLA Ops:
  6.5 9.1 %copy-start = (bf16[5376,256]{1,0:T(8,128)(2,1)S(1)}, bf16[5376,256]{1,0:T(8,128)(2,1)}, u32[]{:S(2)}) copy-start(bf16[5376,256]{1,0:T(8,128)(2,1)} %param.8) | copy-start | bytes 8257540
  6.5 3.9 %copy-start.3 = (f32[5376]{0:T(1024)S(1)}, f32[5376]{0:T(1024)}, u32[]{:S(2)}) copy-start(f32[5376]{0:T(1024)} %param.6) | copy-start | bytes 64516
  6.5 195.8 %reduce-scatter.4.cloned.1.call-start = ((), (), s32[]{:S(2)}) async-start(), calls=%async_computation.1 | async-start | bytes 5734400 | tf_op jit(solution)/shard_map/reduce_scatter | solution.py:74
  10.5 5.2 %copy-start.1 = (bf16[512,5376]{1,0:T(8,128)(2,1)S(1)}, bf16[512,5376]{1,0:T(8,128)(2,1)}, u32[]{:S(2)}) copy-start(bf16[512,5376]{1,0:T(8,128)(2,1)} %param.5) | copy-start | bytes 16515076
  18.3 14.0 %collective-permute-start.1 = (bf16[512,128]{0,1:T(8,128)(2,1)S(1)}, bf16[512,128]{0,1:T(8,128)(2,1)}, u32[]{:S(2)}, u32[]{:S(2)}) collective-permute-start(bf16[512,128]{0,1:T(8,128)(2,1)S(1)} %pad_maximum_fusion), channel_id=1, source_target_pairs={{0,24},{24,48},{48,72},{72,96},{96,120},{120,144},{144,168},{168,1... | collective-permute-start | bytes 393224 | tf_op jit(solution)/shard_map/ppermute | solution.py:14
  20.2 12.1 %collective-permute-start = (bf16[512,128]{0,1:T(8,128)(2,1)S(1)}, bf16[512,128]{0,1:T(8,128)(2,1)}, u32[]{:S(2)}, u32[]{:S(2)}) collective-permute-start(bf16[512,128]{0,1:T(8,128)(2,1)S(1)} %pad_maximum_fusion), channel_id=1, source_target_pairs={{0,48},{24,72},{48,96},{72,120},{96,144},{120,168},{144,192},{168,... | collective-permute-start | bytes 393224 | tf_op jit(solution)/shard_map/ppermute | solution.py:14
  23.3 13.4 %collective-permute-start.3 = (bf16[512,128]{0,1:T(8,128)(2,1)S(1)}, bf16[512,128]{0,1:T(8,128)(2,1)S(1)}, u32[]{:S(2)}, u32[]{:S(2)}) collective-permute-start(bf16[512,128]{0,1:T(8,128)(2,1)S(1)} %slice.38), channel_id=1, source_target_pairs={{0,24},{24,48},{48,72},{72,96},{96,120},{120,144},{144,168},{168,1... | collective-permute-start | bytes 393224 | tf_op jit(solution)/shard_map/ppermute | solution.py:14
  28.8 8.0 %collective-permute-start.2 = (bf16[512,128]{0,1:T(8,128)(2,1)S(1)}, bf16[512,128]{0,1:T(8,128)(2,1)S(1)}, u32[]{:S(2)}, u32[]{:S(2)}) collective-permute-start(bf16[512,128]{0,1:T(8,128)(2,1)S(1)} %slice.38), channel_id=1, source_target_pairs={{0,48},{24,72},{48,96},{72,120},{96,144},{120,168},{144,192},{168,... | collective-permute-start | bytes 393224 | tf_op jit(solution)/shard_map/ppermute | solution.py:14
  34.6 1.7 copy-start.2
Sparse Core Ops, SparseCore 0:
  52.8 149.4 reduce-scatter.3
where the time goes:
time: 210 us; the launch traced here: 209 us
  waiting for transfers between devices  150 us (71%)
  matrix products  17 us (8%)
  starting transfers between devices  13.9 us (7%)
  between operations  13.6 us (6%)
  local copies, waits for them, and re-layouts  9.97 us (5%)
  other arithmetic  5.08 us (2%)
    reduce_scatter x1, waiting for transfers between devices, per_device(): lax.psum_scatter(lax.dot_general(out_weight, outputs, (((0,), (1,)), ((),...  150 us
    ppermute x4, starting transfers between devices, shifted(): return lax.ppermute(block, axis, route)  13.9 us
    unnamed x9, local copies, waits for them, and re-layouts  9.95 us
    dot_general x1, matrix products, per_device(): lax.dot_general(out_weight, outputs, (((0,), (1,)), ((), ())), preferred_...  7.57 us
    dot_general x1, matrix products, per_device(): jnp.dot(normed, query_weight, preferred_element_type=jnp.float32)  5.15 us
  transfers between devices with their start and end apart: 5, of which 1 were waited for; matrix products, arithmetic and copies ran while one was open for 1% of the time, Pallas kernels for 0%

commit v1 on v0

v1 whole, which is shorter than its diff:
```python
import math

import jax
import jax.numpy as jnp
from jax import lax
from jax.experimental import pallas as pl
from jax.experimental.pallas import tpu as pltpu
from jax.sharding import PartitionSpec as P

MESH = pl.DeviceIdType.MESH
BF = jnp.bfloat16
F32 = jnp.float32

D = 5376
HD = 128
WINDOW = 1024
ROWS = 512
NZ = 12
NX = 4
HALF = NZ // 2
FEATS = D // NZ
MINE = FEATS // 2
QUARTER = FEATS // NX
NK = 7
KC = D // NK
NB = 4
BLK = ROWS // NB
KEYS = WINDOW + BLK
SCALE = math.log2(math.e) / math.sqrt(168.0)

NT = (((1,), (1,)), ((), ()))


def kernel(
    x_hbm, gain_ref, wq_hbm, wkv_hbm, wo_hbm, cos_ref, sin_ref, out_ref,
    xb, xg, wqb, wkvb, wob, wt, wbuf, kv, qb, ho, acc, ss, rc, rs, psend, precv, own,
    ld_x, ld_kv, ld_q, ld_o,
    a_s, a_r, b_s, b_r, c1_s, c1_r, c2_s, c2_r,
    p1_s, p1_r, p2_s, p2_r, p3_s, p3_r,
    r_s, l_s, g_r, y_s, y_r,
):
    s = lax.axis_index("seq")
    m = lax.axis_index("mp")
    nseq = lax.axis_size("seq")
    z = m // 2
    yl = m % 2
    core = s % 2
    x = (s // 2) % NX
    partner = m + 1 - 2 * yl
    sibling = s + 1 - 2 * core
    has_prev = s >= 2
    has_next = s < nseq - 2

    def at_z(dist):
        return ((z + dist + NZ) % NZ) * 2 + yl

    def at_x(dist):
        return s + 2 * ((x + dist) % NX - x)

    def copy(src, dst, ssem, rsem, seq, mp):
        return pltpu.make_async_remote_copy(
            src_ref=src, dst_ref=dst, send_sem=ssem, recv_sem=rsem,
            device_id=(seq, mp), device_id_type=MESH,
        )

    load_o = pltpu.make_async_copy(wo_hbm, wob, ld_o)
    load_o.start()
    loads = []
    for k in range(NK):
        lx = pltpu.make_async_copy(x_hbm.at[:, pl.ds(k * KC, KC)], xb.at[k], ld_x.at[k])
        lkv = pltpu.make_async_copy(wkv_hbm.at[pl.ds(k * KC, KC), :], wkvb.at[k], ld_kv.at[k])
        lx.start()
        lkv.start()
        loads.append((lx, lkv))
    load_q = pltpu.make_async_copy(wq_hbm, wqb, ld_q)
    load_q.start()

    barrier = pltpu.get_barrier_semaphore()

    def greet(seq, mp):
        pl.semaphore_signal(barrier, inc=1, device_id=(seq, mp), device_id_type=MESH)

    for dist in range(1, NZ):
        greet(s, at_z(dist))
    for dist in range(1, NX):
        greet(at_x(dist), m)
    greet(sibling, m)
    greet(s, partner)

    @pl.when(has_prev)
    def _():
        greet(s - 2, m)

    @pl.when(has_next)
    def _():
        greet(s + 2, m)

    lane = lax.broadcasted_iota(jnp.int32, (32, HD), 1)
    sign = jnp.where(lane < HD // 2, -1.0, 1.0).astype(F32)
    cos_low = cos_ref[16:48, :]
    sin_low = sin_ref[16:48, :]
    for a in range(16):
        cos_high = cos_ref[a : a + 1, :]
        sin_high = sin_ref[a : a + 1, :]
        rc[32 * a : 32 * a + 32, :] = cos_high * cos_low - sin_high * sin_low
        rs[32 * a : 32 * a + 32, :] = (sin_high * cos_low + cos_high * sin_low) * sign

    @pl.when(s == 0)
    def _():
        kv[:, 0 : 2 * ROWS, :] = jnp.zeros((2, 2 * ROWS, HD), BF)

    @pl.when(s == 1)
    def _():
        kv[:, 0:ROWS, :] = jnp.zeros((2, ROWS, HD), BF)

    load_o.wait()
    for f in range(D // HD):
        wt[f * HD : (f + 1) * HD, :] = wob[:, f * HD : (f + 1) * HD].T

    def scale(k):
        for r in range(0, ROWS, 16):
            wide = xb[k, r : r + 16, :].astype(F32)
            square = wide * wide
            part = square[:, 0:HD]
            for c in range(HD, KC, HD):
                part = part + square[:, c : c + HD]
            if k == 0:
                ss[r : r + 16, :] = part
            else:
                ss[r : r + 16, :] += part
            xg[k, r : r + 16, :] = (wide * gain_ref[:, k * KC : (k + 1) * KC]).astype(BF)

    loads[0][0].wait()
    loads[0][1].wait()
    scale(0)
    for k in range(NK):
        if k + 1 < NK:
            loads[k + 1][0].wait()
            loads[k + 1][1].wait()
            scale(k + 1)
        part = jnp.dot(xg[k], wkvb[k], preferred_element_type=F32)
        if k == 0:
            acc[...] = part
        else:
            acc[...] += part
    inverse = lax.rsqrt(jnp.sum(ss[...], axis=1, keepdims=True) * (1.0 / D) + 1e-06)

    def rope(t):
        return t * rc[...] + pltpu.roll(t, HD // 2, 1) * rs[...]

    kv[0, 2 * ROWS : 3 * ROWS, :] = rope(acc[:, 0:HD] * inverse).astype(BF)
    kv[1, 2 * ROWS : 3 * ROWS, :] = (acc[:, HD : 2 * HD] * inverse).astype(BF)

    pl.semaphore_wait(
        barrier,
        (NZ - 1) + (NX - 1) + 2 + has_prev.astype(jnp.int32) + has_next.astype(jnp.int32),
    )

    def copy_a(j):
        return copy(
            kv.at[yl, pl.ds(2 * ROWS + j * BLK, BLK), :], kv.at[yl, pl.ds(j * BLK, BLK), :],
            a_s.at[j], a_r.at[j], s + 2, m,
        )

    def copy_b(j, half):
        block = kv.at[half, pl.ds(j * BLK, BLK), :]
        return copy(block, block, b_s.at[j], b_r.at[j], s, partner)

    def copy_c1():
        return copy(
            kv.at[:, pl.ds(2 * ROWS, ROWS), :], kv.at[:, pl.ds(ROWS, ROWS), :],
            c1_s.at[0], c1_r.at[0], sibling, m,
        )

    def copy_c2(j, half):
        return copy(
            kv.at[half, pl.ds(j * BLK, BLK), :], kv.at[half, pl.ds(ROWS + j * BLK, BLK), :],
            c2_s.at[half, j], c2_r.at[half, j], sibling, m,
        )

    order = tuple(range(NB - 1, -1, -1))

    @pl.when(has_next)
    def _():
        for j in order:
            copy_a(j).start()

    @pl.when(core == 0)
    def _():
        copy_c1().start()

    def copy_p1(j):
        dist = (j + 1) * (1 - 2 * core)
        plane = (z + dist + NZ) % NZ
        slot = 1 + j + HALF * core
        return copy(
            wt.at[pl.ds(pl.multiple_of(plane * FEATS + x * QUARTER, 16), QUARTER), :],
            wbuf.at[slot, pl.ds(pl.multiple_of(x * QUARTER, 16), QUARTER), :],
            p1_s.at[j], p1_r.at[j], s, plane * 2 + yl,
        )

    for j in range(HALF):
        copy_p1(j).start()
    wbuf[0] = wt[pl.ds(pl.multiple_of(z * FEATS, 16), FEATS), :]

    load_q.wait()
    queries = jnp.dot(xg[0], wqb[0:KC, :], preferred_element_type=F32)
    for k in range(1, NK):
        queries = queries + jnp.dot(
            xg[k], wqb[k * KC : (k + 1) * KC, :], preferred_element_type=F32
        )
    qb[...] = (rope(queries * inverse) * SCALE).astype(BF)

    @pl.when(has_prev & (core == 1))
    def _():
        for j in order:
            copy_a(j).wait_recv()
            copy_b(j, yl).start()
            copy_c2(j, yl).start()
        for j in order:
            copy_b(j, 1 - yl).wait_recv()
            copy_c2(j, 1 - yl).start()

    @pl.when(has_prev & (core == 0))
    def _():
        for j in order:
            copy_a(j).wait_recv()
            copy_b(j, yl).start()
        for j in order:
            copy_b(j, 1 - yl).wait_recv()
            copy_c2(j, yl).wait_recv()
            copy_c2(j, 1 - yl).wait_recv()

    @pl.when(core == 1)
    def _():
        copy_c1().wait_recv()

    right, left = at_z(1), at_z(-1)

    def send_right(b, d):
        return copy(ho.at[b, d], ho.at[b, d + 1], r_s.at[b, d], g_r.at[b, d + 1], s, right)

    def send_left(b, e):
        to = HALF if e == HALF - 1 else HALF + e + 1
        frm = 0 if e == 0 else HALF + e
        return copy(ho.at[b, frm], ho.at[b, to], l_s.at[b, e], g_r.at[b, to], s, left)

    first_key = jnp.maximum(WINDOW - ROWS * s, 0)
    query_row = lax.broadcasted_iota(jnp.int32, (BLK, KEYS), 0)
    key_row = lax.broadcasted_iota(jnp.int32, (BLK, KEYS), 1)
    band = (key_row > query_row) & (key_row <= query_row + WINDOW)
    for b in order:
        start = b * BLK
        scores = lax.dot_general(
            qb[start : start + BLK, :], kv[0, start : start + KEYS, :], NT,
            preferred_element_type=F32,
        )
        scores = jnp.where(band & (key_row + start >= first_key), scores, -1e30)
        weights = jnp.exp2(scores - jnp.max(scores, axis=1, keepdims=True))
        total = jnp.sum(weights, axis=1, keepdims=True)
        mixed = jnp.dot(
            weights.astype(BF), kv[1, start : start + KEYS, :], preferred_element_type=F32
        )
        ho[b, 0] = (mixed / total).astype(BF)
        send_right(b, 0).start()
        send_left(b, 0).start()

    def quarter(slot, dist):
        rows = pl.ds(pl.multiple_of(((x - dist + NX) % NX) * QUARTER, 16), QUARTER)
        return wbuf.at[pl.ds(slot, HALF), rows, :]

    mine = 1 + HALF * core
    other = 1 + HALF * (1 - core)

    def copy_p2(dist):
        return copy(quarter(mine, 0), quarter(mine, 0), p2_s.at[dist], p2_r.at[dist], at_x(dist), m)

    def arrival_p2(dist):
        return copy(quarter(mine, dist), quarter(mine, dist), p2_s.at[dist], p2_r.at[dist], at_x(-dist), m)

    def copy_sib(dist, slot):
        return copy(quarter(slot, dist), quarter(slot, dist), p3_s.at[dist], p3_r.at[dist], sibling, m)

    for j in range(HALF):
        copy_p1(j).wait_recv()
    for dist in range(1, NX):
        copy_p2(dist).start()
    copy_sib(0, mine).start()

    for hop in range(1, HALF):
        for b in order:
            send_right(b, hop - 1).wait_recv()
            if hop + 1 < HALF or b < NB // 2:
                send_right(b, hop).start()
            send_left(b, hop - 1).wait_recv()
            if hop + 1 < HALF or b >= NB // 2:
                send_left(b, hop).start()
        if hop == 3:
            for dist in range(1, NX):
                arrival_p2(dist).wait_recv()
                copy_sib(dist, mine).start()
    for dist in range(NX):
        copy_sib(dist, other).wait_recv()

    def copy_y(b):
        return copy(psend.at[b], precv.at[b], y_s.at[b], y_r.at[b], s, partner)

    theirs_at = pl.multiple_of((1 - yl) * MINE, 16)
    mine_at = pl.multiple_of(yl * MINE, 16)

    def product(heads, at):
        rows = jnp.concatenate([wbuf[i, pl.ds(at, MINE), :] for i in range(NZ)], axis=1)
        return lax.dot_general(rows, heads, NT, preferred_element_type=F32)

    for b in order:
        if b < NB // 2:
            send_right(b, HALF - 1).wait_recv()
        else:
            send_left(b, HALF - 1).wait_recv()
        heads = jnp.concatenate([ho[b, i] for i in range(NZ)], axis=1)
        psend[b] = product(heads, theirs_at).astype(BF)
        copy_y(b).start()
        own[b] = product(heads, mine_at)
    for b in order:
        copy_y(b).wait_recv()
        out_ref[:, b * BLK : (b + 1) * BLK] = (own[b] + precv[b].astype(F32)).astype(BF)

    @pl.when(has_next)
    def _():
        for j in order:
            copy_a(j).wait_send()

    @pl.when(core == 0)
    def _():
        copy_c1().wait_send()

    @pl.when(has_prev)
    def _():
        for j in order:
            copy_b(j, yl).wait_send()

    @pl.when(has_prev & (core == 1))
    def _():
        for j in order:
            copy_c2(j, yl).wait_send()
            copy_c2(j, 1 - yl).wait_send()

    for j in range(HALF):
        copy_p1(j).wait_send()
    for dist in range(1, NX):
        copy_p2(dist).wait_send()
    for dist in range(NX):
        copy_sib(dist, mine).wait_send()
    for b in order:
        for hop in range(HALF):
            if hop + 1 < HALF or b < NB // 2:
                send_right(b, hop).wait_send()
            if hop + 1 < HALF or b >= NB // 2:
                send_left(b, hop).wait_send()
        copy_y(b).wait_send()


def per_device(hidden_in, norm_gain, query_weight, kv_weight, out_weight):
    first = (lax.axis_index("seq") * ROWS).astype(F32)
    row = jnp.arange(48, dtype=jnp.int32)
    place = jnp.where(row < 16, first + 32.0 * row.astype(F32), (row - 16).astype(F32))
    index = (jnp.arange(HD, dtype=jnp.int32) % (HD // 2)).astype(F32)
    angle = place[:, None] * jnp.exp(-math.log(10000.0) * index * (2.0 / HD))[None, :]
    any_space = pl.BlockSpec(memory_space=pl.ANY)
    vmem = pl.BlockSpec(memory_space=pltpu.VMEM)
    dma = pltpu.SemaphoreType.DMA
    return pl.pallas_call(
        kernel,
        out_shape=jax.ShapeDtypeStruct((MINE, ROWS), BF),
        in_specs=[any_space, vmem, any_space, any_space, any_space, vmem, vmem],
        out_specs=vmem,
        scratch_shapes=[
            pltpu.VMEM((NK, ROWS, KC), BF),
            pltpu.VMEM((NK, ROWS, KC), BF),
            pltpu.VMEM((D, HD), BF),
            pltpu.VMEM((NK, KC, 2 * HD), BF),
            pltpu.VMEM((HD, D), BF),
            pltpu.VMEM((D, HD), BF),
            pltpu.VMEM((NZ + 1, FEATS, HD), BF),
            pltpu.VMEM((2, 3 * ROWS, HD), BF),
            pltpu.VMEM((ROWS, HD), BF),
            pltpu.VMEM((NB, NZ, BLK, HD), BF),
            pltpu.VMEM((ROWS, 2 * HD), F32),
            pltpu.VMEM((ROWS, HD), F32),
            pltpu.VMEM((ROWS, HD), F32),
            pltpu.VMEM((ROWS, HD), F32),
            pltpu.VMEM((NB, MINE, BLK), BF),
            pltpu.VMEM((NB, MINE, BLK), BF),
            pltpu.VMEM((NB, MINE, BLK), F32),
            dma((NK,)), dma((NK,)), dma, dma,
            dma((NB,)), dma((NB,)), dma((NB,)), dma((NB,)),
            dma((1,)), dma((1,)), dma((2, NB)), dma((2, NB)),
            dma((HALF,)), dma((HALF,)), dma((NX,)), dma((NX,)), dma((NX,)), dma((NX,)),
            dma((NB, HALF)), dma((NB, HALF)), dma((NB, NZ)), dma((NB,)), dma((NB,)),
        ],
        compiler_params=pltpu.CompilerParams(
            collective_id=0, has_side_effects=True, vmem_limit_bytes=60 * 1024 * 1024
        ),
    )(
        hidden_in, norm_gain.reshape(1, D), query_weight, kv_weight, out_weight,
        jnp.cos(angle), jnp.sin(angle),
    )


def solution(mesh):
    in_specs = (P("seq", None), P(), P(None, "mp"), P(None, "mp"), P("mp", None))
    out_specs = P("mp", "seq")
    return jax.shard_map(
        per_device, mesh=mesh, in_specs=in_specs, out_specs=out_specs, check_vma=False
    )
```

time: 210 us -> 66.7 us (0.32)
  the two profiles are of different devices: /device:TPU:20 before, /device:TPU:56 now
where the time goes in v1:
time: 66.7 us; the launch traced here: 66.5 us
  Pallas kernels  62.7 us (94%)
  local copies, waits for them, and re-layouts  3 us (4%)
  other arithmetic  0.8 us (1%)
    pallas_call x1, Pallas kernels, per_device(): pl.pallas_call(kernel, out_shape=jax.ShapeDtypeStruct((MINE, ROWS), BF),...  62.7 us
    unnamed x1, local copies, waits for them, and re-layouts  1.64 us
    reshape x1, local copies, waits for them, and re-layouts, per_device(): norm_gain.reshape(1, D)  1.36 us

profile of v1, /device:TPU:56, one launch (start us, length us, event | category | flops | bytes accessed | tf_op | source)
XLA Modules:
  0.0 66.5 jit_solution(6997905429976600048)
XLA Ops:
  0.0 1.4 %reshape.27.gain_ref = f32[1,5376]{1,0:T(1,128)} reshape(f32[5376]{0:T(1024)} %param.6) | data formatting | bytes 43008 | tf_op jit(solution)/shard_map/reshape | solution.py:405
  1.4 0.8 %multiply_sine_fusion = (f32[48,128]{1,0:T(8,128)}, f32[48,128]{1,0:T(8,128)}) fusion(f32[128]{0:T(128)S(1)} %fusion.2, f32[48]{0:T(128)S(1)} %compare_select_fusion), kind=kLoop, calls=%fused_computation | loop fusion | flops 6144 | bytes 49856 | tf_op jit(solution)/shard_map/sin | solution.py:406
  2.2 62.7 %shard_map.55 = bf16[224,512]{1,0:T(8,128)(2,1)} custom-call(bf16[512,5376]{1,0:T(8,128)(2,1)} %x_hbm.1, f32[1,5376]{1,0:T(1,128)} %reshape.27.gain_ref, bf16[5376,128]{1,0:T(8,128)(2,1)} %wq_hbm.1, bf16[5376,256]{1,0:T(8,128)(2,1)} %wkv_hbm.1, bf16[128,5376]{1,0:T(8,128)(2,1)} %wo_hbm.1, f32[48,128]{1,0:T(8,128)} %get-tuple-element.6.cos_ref, ...), custom_call_target="tpu_custom_call" | custom-call | tf_op jit(solution)/shard_map/pallas_call | solution.py:372
  64.8 1.6 %copy.7 = bf16[224,512]{1,0:T(8,128)(2,1)} copy(bf16[224,512]{1,0:T(8,128)(2,1)} %shard_map.55) | data formatting | bytes 458752
  (2 shorter events, 0.0 us)

commit v2 on v1

--- a/solution.py
+++ b/solution.py
@@ -2,6 +2,7 @@
 
 import jax
 import jax.numpy as jnp
+import numpy as np
 from jax import lax
 from jax.experimental import pallas as pl
 from jax.experimental.pallas import tpu as pltpu
@@ -23,6 +24,7 @@
 QUARTER = FEATS // NX
 NK = 7
 KC = D // NK
+AHEAD = 4
 NB = 4
 BLK = ROWS // NB
 KEYS = WINDOW + BLK
@@ -32,12 +34,12 @@
 
 
 def kernel(
-    x_hbm, gain_ref, wq_hbm, wkv_hbm, wo_hbm, cos_ref, sin_ref, out_ref,
-    xb, xg, wqb, wkvb, wob, wt, wbuf, kv, qb, ho, acc, ss, rc, rs, psend, precv, own,
+    x_hbm, gain_ref, wq_hbm, wkv_hbm, wo_hbm, freq_ref, out_ref,
+    xb, xg, wqb, wkvb, wob, wt, wbuf, kv, qb, ho, acc, ss, rc, rs, psend, precv, own, rel,
     ld_x, ld_kv, ld_q, ld_o,
     a_s, a_r, b_s, b_r, c1_s, c1_r, c2_s, c2_r,
     p1_s, p1_r, p2_s, p2_r, p3_s, p3_r,
-    r_s, l_s, g_r, y_s, y_r,
+    r_s, l_s, g_r, y_s, y_r, f_s, f_r,
 ):
     s = lax.axis_index("seq")
     m = lax.axis_index("mp")
@@ -50,6 +52,9 @@
     sibling = s + 1 - 2 * core
     has_prev = s >= 2
     has_next = s < nseq - 2
+    turns = x == NX - 1
+    passes = (x == 0) & (s < nseq - 2 * NX) & (yl == 1)
+    passed = (x == 0) & has_prev & (yl == 0)
 
     def at_z(dist):
         return ((z + dist + NZ) % NZ) * 2 + yl
@@ -64,16 +69,25 @@
         )
 
     load_o = pltpu.make_async_copy(wo_hbm, wob, ld_o)
-    load_o.start()
-    loads = []
-    for k in range(NK):
-        lx = pltpu.make_async_copy(x_hbm.at[:, pl.ds(k * KC, KC)], xb.at[k], ld_x.at[k])
-        lkv = pltpu.make_async_copy(wkv_hbm.at[pl.ds(k * KC, KC), :], wkvb.at[k], ld_kv.at[k])
-        lx.start()
-        lkv.start()
-        loads.append((lx, lkv))
     load_q = pltpu.make_async_copy(wq_hbm, wqb, ld_q)
-    load_q.start()
+
+    def load_x(k):
+        return pltpu.make_async_copy(x_hbm.at[:, pl.ds(k * KC, KC)], xb.at[k], ld_x.at[k])
+
+    def load_kv(k):
+        return pltpu.make_async_copy(wkv_hbm.at[pl.ds(k * KC, KC), :], wkvb.at[k], ld_kv.at[k])
+
+    def load(k):
+        if k < NK:
+            load_x(k).start()
+            load_kv(k).start()
+        elif k == NK:
+            load_o.start()
+        elif k == NK + 1:
+            load_q.start()
+
+    for k in range(AHEAD):
+        load(k)
 
     barrier = pltpu.get_barrier_semaphore()
 
@@ -95,13 +109,26 @@
     def _():
         greet(s + 2, m)
 
+    @pl.when(passes)
+    def _():
+        greet(s + 2 * NX, m - 1)
+
+    @pl.when(passed)
+    def _():
+        greet(s - 2 * NX, m + 1)
+
     lane = lax.broadcasted_iota(jnp.int32, (32, HD), 1)
     sign = jnp.where(lane < HD // 2, -1.0, 1.0).astype(F32)
-    cos_low = cos_ref[16:48, :]
-    sin_low = sin_ref[16:48, :]
+    row = lax.broadcasted_iota(jnp.int32, (48, HD), 0)
+    place = jnp.where(row < 16, ROWS * s + 32 * row, row - 16).astype(F32)
+    angle = place * freq_ref[...]
+    cosine = jnp.cos(angle)
+    sine = jnp.sin(angle)
+    cos_low = cosine[16:48, :]
+    sin_low = sine[16:48, :]
     for a in range(16):
-        cos_high = cos_ref[a : a + 1, :]
-        sin_high = sin_ref[a : a + 1, :]
+        cos_high = cosine[a : a + 1, :]
+        sin_high = sine[a : a + 1, :]
         rc[32 * a : 32 * a + 32, :] = cos_high * cos_low - sin_high * sin_low
         rs[32 * a : 32 * a + 32, :] = (sin_high * cos_low + cos_high * sin_low) * sign
 
@@ -113,11 +140,8 @@
     def _():
         kv[:, 0:ROWS, :] = jnp.zeros((2, ROWS, HD), BF)
 
-    load_o.wait()
-    for f in range(D // HD):
-        wt[f * HD : (f + 1) * HD, :] = wob[:, f * HD : (f + 1) * HD].T
-
     def scale(k):
+        gain = gain_ref[pl.ds(k * KC, KC)].reshape(1, KC)
         for r in range(0, ROWS, 16):
             wide = xb[k, r : r + 16, :].astype(F32)
             square = wide * wide
@@ -128,15 +152,18 @@
                 ss[r : r + 16, :] = part
             else:
                 ss[r : r + 16, :] += part
-            xg[k, r : r + 16, :] = (wide * gain_ref[:, k * KC : (k + 1) * KC]).astype(BF)
-
-    loads[0][0].wait()
-    loads[0][1].wait()
+            xg[k, r : r + 16, :] = (wide * gain).astype(BF)
+
+    def arrive(k):
+        load_x(k).wait()
+        load_kv(k).wait()
+        load(k + AHEAD)
+
+    arrive(0)
     scale(0)
     for k in range(NK):
         if k + 1 < NK:
-            loads[k + 1][0].wait()
-            loads[k + 1][1].wait()
+            arrive(k + 1)
             scale(k + 1)
         part = jnp.dot(xg[k], wkvb[k], preferred_element_type=F32)
         if k == 0:
@@ -153,7 +180,8 @@
 
     pl.semaphore_wait(
         barrier,
-        (NZ - 1) + (NX - 1) + 2 + has_prev.astype(jnp.int32) + has_next.astype(jnp.int32),
+        (NZ - 1) + (NX - 1) + 2 + has_prev.astype(jnp.int32) + has_next.astype(jnp.int32)
+        + passes.astype(jnp.int32) + passed.astype(jnp.int32),
     )
 
     def copy_a(j):
@@ -180,14 +208,42 @@
 
     order = tuple(range(NB - 1, -1, -1))
 
-    @pl.when(has_next)
-    def _():
-        for j in order:
-            copy_a(j).start()
+    def copy_in(j):
+        return copy(
+            kv.at[0, pl.ds(2 * ROWS + j * BLK, BLK), :], rel.at[j], f_s.at[0, j], f_r.at[j], at_x(1), m,
+        )
+
+    def copy_on(j):
+        return copy(
+            rel.at[j], kv.at[0, pl.ds(j * BLK, BLK), :], f_s.at[1, j], a_r.at[j], s + 2 * NX, m - 1,
+        )
+
+    straight = has_next & (jnp.logical_not(turns) | (yl == 1))
+    around = has_next & turns & (yl == 1)
+
+    def send_on(which):
+        @pl.when(straight)
+        def _():
+            for j in which:
+                copy_a(j).start()
+
+        @pl.when(around)
+        def _():
+            for j in which:
+                copy_in(j).start()
+
+    @pl.when(core == 1)
+    def _():
+        send_on(order)
 
     @pl.when(core == 0)
     def _():
+        send_on(order[:1])
         copy_c1().start()
+
+    load_o.wait()
+    for f in range(D // HD):
+        wt[f * HD : (f + 1) * HD, :] = wob[:, f * HD : (f + 1) * HD].T
 
     def copy_p1(j):
         dist = (j + 1) * (1 - 2 * core)
@@ -211,6 +267,16 @@
         )
     qb[...] = (rope(queries * inverse) * SCALE).astype(BF)
 
+    @pl.when(core == 0)
+    def _():
+        send_on(order[1:])
+
+    @pl.when(passes)
+    def _():
+        for j in order:
+            copy_in(j).wait_recv()
+            copy_on(j).start()
+
     @pl.when(has_prev & (core == 1))
     def _():
         for j in order:
@@ -227,7 +293,6 @@
             copy_a(j).wait_recv()
             copy_b(j, yl).start()
         for j in order:
-            copy_b(j, 1 - yl).wait_recv()
             copy_c2(j, yl).wait_recv()
             copy_c2(j, 1 - yl).wait_recv()
 
@@ -246,16 +311,30 @@
         return copy(ho.at[b, frm], ho.at[b, to], l_s.at[b, e], g_r.at[b, to], s, left)
 
     first_key = jnp.maximum(WINDOW - ROWS * s, 0)
-    query_row = lax.broadcasted_iota(jnp.int32, (BLK, KEYS), 0)
-    key_row = lax.broadcasted_iota(jnp.int32, (BLK, KEYS), 1)
-    band = (key_row > query_row) & (key_row <= query_row + WINDOW)
+    query_row = lax.broadcasted_iota(jnp.int32, (BLK, BLK), 0)
+    key_row = lax.broadcasted_iota(jnp.int32, (BLK, BLK), 1)
+    column = lax.broadcasted_iota(jnp.int32, (1, KEYS), 1)
     for b in order:
         start = b * BLK
+
+        @pl.when(has_prev & (core == 0))
+        def _():
+            copy_b(b, 1 - yl).wait_recv()
+
         scores = lax.dot_general(
             qb[start : start + BLK, :], kv[0, start : start + KEYS, :], NT,
             preferred_element_type=F32,
         )
-        scores = jnp.where(band & (key_row + start >= first_key), scores, -1e30)
+        exists = column + start >= first_key
+        scores = jnp.where(exists, scores, -1e30)
+        scores = jnp.concatenate(
+            [
+                jnp.where(key_row > query_row, scores[:, 0:BLK], -1e30),
+                scores[:, BLK:WINDOW],
+                jnp.where(key_row <= query_row, scores[:, WINDOW:KEYS], -1e30),
+            ],
+            axis=1,
+        )
         weights = jnp.exp2(scores - jnp.max(scores, axis=1, keepdims=True))
         total = jnp.sum(weights, axis=1, keepdims=True)
         mixed = jnp.dot(
@@ -308,27 +387,40 @@
     theirs_at = pl.multiple_of((1 - yl) * MINE, 16)
     mine_at = pl.multiple_of(yl * MINE, 16)
 
-    def product(heads, at):
-        rows = jnp.concatenate([wbuf[i, pl.ds(at, MINE), :] for i in range(NZ)], axis=1)
+    def product(b, slots, at):
+        rows = jnp.concatenate([wbuf[i, pl.ds(at, MINE), :] for i in slots], axis=1)
+        heads = jnp.concatenate([ho[b, i] for i in slots], axis=1)
         return lax.dot_general(rows, heads, NT, preferred_element_type=F32)
 
+    early = [i for i in range(NZ) if i != HALF]
     for b in order:
+        theirs = product(b, early, theirs_at)
+        mine_part = product(b, early, mine_at)
         if b < NB // 2:
             send_right(b, HALF - 1).wait_recv()
         else:
             send_left(b, HALF - 1).wait_recv()
-        heads = jnp.concatenate([ho[b, i] for i in range(NZ)], axis=1)
-        psend[b] = product(heads, theirs_at).astype(BF)
+        psend[b] = (theirs + product(b, [HALF], theirs_at)).astype(BF)
         copy_y(b).start()
-        own[b] = product(heads, mine_at)
+        own[b] = mine_part + product(b, [HALF], mine_at)
     for b in order:
         copy_y(b).wait_recv()
         out_ref[:, b * BLK : (b + 1) * BLK] = (own[b] + precv[b].astype(F32)).astype(BF)
 
-    @pl.when(has_next)
+    @pl.when(straight)
     def _():
         for j in order:
             copy_a(j).wait_send()
+
+    @pl.when(around)
+    def _():
+        for j in order:
+            copy_in(j).wait_send()
+
+    @pl.when(passes)
+    def _():
+        for j in order:
+            copy_on(j).wait_send()
 
     @pl.when(core == 0)
     def _():
@@ -361,18 +453,15 @@
 
 
 def per_device(hidden_in, norm_gain, query_weight, kv_weight, out_weight):
-    first = (lax.axis_index("seq") * ROWS).astype(F32)
-    row = jnp.arange(48, dtype=jnp.int32)
-    place = jnp.where(row < 16, first + 32.0 * row.astype(F32), (row - 16).astype(F32))
-    index = (jnp.arange(HD, dtype=jnp.int32) % (HD // 2)).astype(F32)
-    angle = place[:, None] * jnp.exp(-math.log(10000.0) * index * (2.0 / HD))[None, :]
+    index = np.arange(HD) % (HD // 2)
+    freq = np.exp(-math.log(10000.0) * index * (2.0 / HD)).astype(np.float32)[None, :]
     any_space = pl.BlockSpec(memory_space=pl.ANY)
     vmem = pl.BlockSpec(memory_space=pltpu.VMEM)
     dma = pltpu.SemaphoreType.DMA
     return pl.pallas_call(
         kernel,
         out_shape=jax.ShapeDtypeStruct((MINE, ROWS), BF),
-        in_specs=[any_space, vmem, any_space, any_space, any_space, vmem, vmem],
+        in_specs=[any_space, vmem, any_space, any_space, any_space, vmem],
         out_specs=vmem,
         scratch_shapes=[
             pltpu.VMEM((NK, ROWS, KC), BF),
@@ -392,18 +481,19 @@
             pltpu.VMEM((NB, MINE, BLK), BF),
             pltpu.VMEM((NB, MINE, BLK), BF),
             pltpu.VMEM((NB, MINE, BLK), F32),
+            pltpu.VMEM((NB, BLK, HD), BF),
             dma((NK,)), dma((NK,)), dma, dma,
             dma((NB,)), dma((NB,)), dma((NB,)), dma((NB,)),
             dma((1,)), dma((1,)), dma((2, NB)), dma((2, NB)),
             dma((HALF,)), dma((HALF,)), dma((NX,)), dma((NX,)), dma((NX,)), dma((NX,)),
             dma((NB, HALF)), dma((NB, HALF)), dma((NB, NZ)), dma((NB,)), dma((NB,)),
+            dma((2, NB)), dma((NB,)),
         ],
         compiler_params=pltpu.CompilerParams(
             collective_id=0, has_side_effects=True, vmem_limit_bytes=60 * 1024 * 1024
         ),
     )(
-        hidden_in, norm_gain.reshape(1, D), query_weight, kv_weight, out_weight,
-        jnp.cos(angle), jnp.sin(angle),
+        hidden_in, norm_gain, query_weight, kv_weight, out_weight, jnp.asarray(freq),
     )
 
 

time: 66.7 us -> 62.6 us (0.939)
  the two profiles are of different devices: /device:TPU:56 before, /device:TPU:48 now
where the time goes in v2:
time: 62.6 us; the launch traced here: 62.4 us
  Pallas kernels  60.7 us (97%)
  local copies, waits for them, and re-layouts  1.64 us (3%)
    pallas_call x1, Pallas kernels, per_device(): pl.pallas_call(kernel, out_shape=jax.ShapeDtypeStruct((MINE, ROWS), BF),...  60.7 us
    unnamed x1, local copies, waits for them, and re-layouts  1.64 us

profile of v2, /device:TPU:48, one launch (start us, length us, event | category | flops | bytes accessed | tf_op | source)
XLA Modules:
  0.0 62.4 jit_solution(12160883836148856862)
XLA Ops:
  0.0 60.7 %shard_map.64 = bf16[224,512]{1,0:T(8,128)(2,1)} custom-call(bf16[512,5376]{1,0:T(8,128)(2,1)} %x_hbm.1, f32[5376]{0:T(1024)} %gain_ref.1, bf16[5376,128]{1,0:T(8,128)(2,1)} %wq_hbm.1, bf16[5376,256]{1,0:T(8,128)(2,1)} %wkv_hbm.1, bf16[128,5376]{1,0:T(8,128)(2,1)} %wo_hbm.1, f32[1,128]{1,0:T(1,128)} %constant.2.clone.freq_ref), custom_call_target="tpu_custom_call" | custom-call | tf_op jit(solution)/shard_map/pallas_call | solution.py:461
  60.7 1.6 %copy.8 = bf16[224,512]{1,0:T(8,128)(2,1)} copy(bf16[224,512]{1,0:T(8,128)(2,1)} %shard_map.64) | data formatting | bytes 458752

commit v3 on v2

--- a/solution.py
+++ b/solution.py
@@ -271,6 +271,31 @@
     def _():
         send_on(order[1:])
 
+    def quarter(slot, dist):
+        rows = pl.ds(pl.multiple_of(((x - dist + NX) % NX) * QUARTER, 16), QUARTER)
+        return wbuf.at[pl.ds(slot, HALF), rows, :]
+
+    mine = 1 + HALF * core
+    other = 1 + HALF * (1 - core)
+
+    def copy_p2(dist):
+        return copy(quarter(mine, 0), quarter(mine, 0), p2_s.at[dist], p2_r.at[dist], at_x(dist), m)
+
+    def arrival_p2(dist):
+        return copy(quarter(mine, dist), quarter(mine, dist), p2_s.at[dist], p2_r.at[dist], at_x(-dist), m)
+
+    def copy_sib(dist, slot):
+        return copy(quarter(slot, dist), quarter(slot, dist), p3_s.at[dist], p3_r.at[dist], sibling, m)
+
+    def spread():
+        for j in range(HALF):
+            copy_p1(j).wait_recv()
+        for dist in (2, 1, 3):
+            copy_p2(dist).start()
+        copy_sib(0, mine).start()
+
+    late = has_prev & (x == 0)
+
     @pl.when(passes)
     def _():
         for j in order:
@@ -283,6 +308,11 @@
             copy_a(j).wait_recv()
             copy_b(j, yl).start()
             copy_c2(j, yl).start()
+
+        @pl.when(late)
+        def _():
+            spread()
+
         for j in order:
             copy_b(j, 1 - yl).wait_recv()
             copy_c2(j, 1 - yl).start()
@@ -292,6 +322,11 @@
         for j in order:
             copy_a(j).wait_recv()
             copy_b(j, yl).start()
+
+        @pl.when(late)
+        def _():
+            spread()
+
         for j in order:
             copy_c2(j, yl).wait_recv()
             copy_c2(j, 1 - yl).wait_recv()
@@ -344,27 +379,9 @@
         send_right(b, 0).start()
         send_left(b, 0).start()
 
-    def quarter(slot, dist):
-        rows = pl.ds(pl.multiple_of(((x - dist + NX) % NX) * QUARTER, 16), QUARTER)
-        return wbuf.at[pl.ds(slot, HALF), rows, :]
-
-    mine = 1 + HALF * core
-    other = 1 + HALF * (1 - core)
-
-    def copy_p2(dist):
-        return copy(quarter(mine, 0), quarter(mine, 0), p2_s.at[dist], p2_r.at[dist], at_x(dist), m)
-
-    def arrival_p2(dist):
-        return copy(quarter(mine, dist), quarter(mine, dist), p2_s.at[dist], p2_r.at[dist], at_x(-dist), m)
-
-    def copy_sib(dist, slot):
-        return copy(quarter(slot, dist), quarter(slot, dist), p3_s.at[dist], p3_r.at[dist], sibling, m)
-
-    for j in range(HALF):
-        copy_p1(j).wait_recv()
-    for dist in range(1, NX):
-        copy_p2(dist).start()
-    copy_sib(0, mine).start()
+    @pl.when(jnp.logical_not(late))
+    def _():
+        spread()
 
     for hop in range(1, HALF):
         for b in order:
@@ -374,10 +391,9 @@
             send_left(b, hop - 1).wait_recv()
             if hop + 1 < HALF or b >= NB // 2:
                 send_left(b, hop).start()
-        if hop == 3:
-            for dist in range(1, NX):
-                arrival_p2(dist).wait_recv()
-                copy_sib(dist, mine).start()
+    for dist in range(1, NX):
+        arrival_p2(dist).wait_recv()
+        copy_sib(dist, mine).start()
     for dist in range(NX):
         copy_sib(dist, other).wait_recv()
 

time: 62.6 us -> 63.9 us (1.021)
  Pallas kernels: 60.7 us -> 61.6 us
    pallas_call x1, Pallas kernels: 60.7 us -> 61.6 us  [per_device(): pl.pallas_call(kernel, out_shape=jax.ShapeDtypeStruct((MINE, ROWS), BF),...]
where the time goes in v3:
time: 63.9 us; the launch traced here: 63.3 us
  Pallas kernels  61.6 us (96%)
  local copies, waits for them, and re-layouts  1.64 us (3%)
    pallas_call x1, Pallas kernels, per_device(): pl.pallas_call(kernel, out_shape=jax.ShapeDtypeStruct((MINE, ROWS), BF),...  61.6 us
    unnamed x1, local copies, waits for them, and re-layouts  1.64 us

profile of v3, /device:TPU:48, one launch (start us, length us, event | category | flops | bytes accessed | tf_op | source)
XLA Modules:
  0.0 63.3 jit_solution(2415909973281728832)
XLA Ops:
  0.0 61.6 %shard_map.64 = bf16[224,512]{1,0:T(8,128)(2,1)} custom-call(bf16[512,5376]{1,0:T(8,128)(2,1)} %x_hbm.1, f32[5376]{0:T(1024)} %gain_ref.1, bf16[5376,128]{1,0:T(8,128)(2,1)} %wq_hbm.1, bf16[5376,256]{1,0:T(8,128)(2,1)} %wkv_hbm.1, bf16[128,5376]{1,0:T(8,128)(2,1)} %wo_hbm.1, f32[1,128]{1,0:T(1,128)} %constant.2.clone.freq_ref), custom_call_target="tpu_custom_call" | custom-call | tf_op jit(solution)/shard_map/pallas_call | solution.py:477
  61.6 1.6 %copy.8 = bf16[224,512]{1,0:T(8,128)(2,1)} copy(bf16[224,512]{1,0:T(8,128)(2,1)} %shard_map.64) | data formatting | bytes 458752

commit v4 on v3

--- a/solution.py
+++ b/solution.py
@@ -35,11 +35,12 @@
 
 def kernel(
     x_hbm, gain_ref, wq_hbm, wkv_hbm, wo_hbm, freq_ref, out_ref,
-    xb, xg, wqb, wkvb, wob, wt, wbuf, kv, qb, ho, acc, ss, rc, rs, psend, precv, own, rel,
+    xb, xg, wqb, wkvb, wob, wt, wbuf, kv, qb, ho, acc, ss, rc, rs, psend, precv, own, rel, h2,
     ld_x, ld_kv, ld_q, ld_o,
     a_s, a_r, b_s, b_r, c1_s, c1_r, c2_s, c2_r,
     p1_s, p1_r, p2_s, p2_r, p3_s, p3_r,
     r_s, l_s, g_r, y_s, y_r, f_s, f_r,
+    r2_s, l2_s, g2_r, d_s,
 ):
     s = lax.axis_index("seq")
     m = lax.axis_index("mp")
@@ -99,6 +100,8 @@
     for dist in range(1, NX):
         greet(at_x(dist), m)
     greet(sibling, m)
+    greet(sibling, at_z(1))
+    greet(sibling, at_z(-1))
     greet(s, partner)
 
     @pl.when(has_prev)
@@ -180,7 +183,7 @@
 
     pl.semaphore_wait(
         barrier,
-        (NZ - 1) + (NX - 1) + 2 + has_prev.astype(jnp.int32) + has_next.astype(jnp.int32)
+        (NZ - 1) + (NX - 1) + 4 + has_prev.astype(jnp.int32) + has_next.astype(jnp.int32)
         + passes.astype(jnp.int32) + passed.astype(jnp.int32),
     )
 
@@ -344,6 +347,28 @@
         to = HALF if e == HALF - 1 else HALF + e + 1
         frm = 0 if e == 0 else HALF + e
         return copy(ho.at[b, frm], ho.at[b, to], l_s.at[b, e], g_r.at[b, to], s, left)
+
+    def send_right2(b, d):
+        return copy(h2.at[b, d], h2.at[b, d + 1], r2_s.at[b, d], g2_r.at[b, d + 1], s, right)
+
+    def send_left2(b, e):
+        to = HALF if e == HALF - 1 else HALF + e + 1
+        return copy(h2.at[b, HALF + e], h2.at[b, to], l2_s.at[b, e], g2_r.at[b, to], s, left)
+
+    def enter_right(b):
+        return copy(ho.at[b, 0], h2.at[b, 1], r2_s.at[b, 0], g2_r.at[b, 1], sibling, right)
+
+    def enter_left(b):
+        return copy(ho.at[b, 0], h2.at[b, HALF + 1], l2_s.at[b, 0], g2_r.at[b, HALF + 1], sibling, left)
+
+    def hand(b, i):
+        return copy(h2.at[b, i], ho.at[b, i], d_s.at[b, i], g_r.at[b, i], sibling, m)
+
+    def goes_right(b, hop):
+        return hop + 1 < HALF or b < NB // 2
+
+    def goes_left(b, hop):
+        return hop + 1 < HALF or b >= NB // 2
 
     first_key = jnp.maximum(WINDOW - ROWS * s, 0)
     query_row = lax.broadcasted_iota(jnp.int32, (BLK, BLK), 0)
@@ -376,24 +401,68 @@
             weights.astype(BF), kv[1, start : start + KEYS, :], preferred_element_type=F32
         )
         ho[b, 0] = (mixed / total).astype(BF)
-        send_right(b, 0).start()
-        send_left(b, 0).start()
+
+        @pl.when(core == 1)
+        def _():
+            send_right(b, 0).start()
+            send_left(b, 0).start()
+
+        @pl.when(core == 0)
+        def _():
+            enter_right(b).start()
+            enter_left(b).start()
+
 
     @pl.when(jnp.logical_not(late))
     def _():
         spread()
 
-    for hop in range(1, HALF):
+    def step(hop):
         for b in order:
             send_right(b, hop - 1).wait_recv()
-            if hop + 1 < HALF or b < NB // 2:
+            if goes_right(b, hop):
                 send_right(b, hop).start()
             send_left(b, hop - 1).wait_recv()
-            if hop + 1 < HALF or b >= NB // 2:
+            if goes_left(b, hop):
                 send_left(b, hop).start()
-    for dist in range(1, NX):
-        arrival_p2(dist).wait_recv()
-        copy_sib(dist, mine).start()
+
+    def step2(hop):
+        for b in order:
+            send_right2(b, hop - 1).wait_recv()
+            if goes_right(b, hop):
+                send_right2(b, hop).start()
+            hand(b, hop).start()
+            send_left2(b, hop - 1).wait_recv()
+            if goes_left(b, hop):
+                send_left2(b, hop).start()
+            hand(b, HALF + hop).start()
+
+    def spread_on():
+        for dist in range(1, NX):
+            arrival_p2(dist).wait_recv()
+            copy_sib(dist, mine).start()
+
+    @pl.when(core == 1)
+    def _():
+        step(1)
+        for hop in range(1, HALF):
+            if hop + 1 < HALF:
+                step(hop + 1)
+            step2(hop)
+            if hop == HALF - 2:
+                spread_on()
+        for b in order:
+            send_right2(b, HALF - 1).wait_recv()
+            hand(b, HALF).start()
+
+    @pl.when(core == 0)
+    def _():
+        spread_on()
+        for b in order:
+            for i in range(1, NZ):
+                if i != HALF:
+                    hand(b, i).wait_recv()
+
     for dist in range(NX):
         copy_sib(dist, other).wait_recv()
 
@@ -412,10 +481,7 @@
     for b in order:
         theirs = product(b, early, theirs_at)
         mine_part = product(b, early, mine_at)
-        if b < NB // 2:
-            send_right(b, HALF - 1).wait_recv()
-        else:
-            send_left(b, HALF - 1).wait_recv()
+        hand(b, HALF).wait_recv()
         psend[b] = (theirs + product(b, [HALF], theirs_at)).astype(BF)
         copy_y(b).start()
         own[b] = mine_part + product(b, [HALF], mine_at)
@@ -459,12 +525,28 @@
         copy_p2(dist).wait_send()
     for dist in range(NX):
         copy_sib(dist, mine).wait_send()
+    @pl.when(core == 1)
+    def _():
+        for b in order:
+            for hop in range(HALF):
+                if goes_right(b, hop):
+                    send_right(b, hop).wait_send()
+                    if hop > 0:
+                        send_right2(b, hop).wait_send()
+                if goes_left(b, hop):
+                    send_left(b, hop).wait_send()
+                    if hop > 0:
+                        send_left2(b, hop).wait_send()
+            for i in range(1, NZ):
+                hand(b, i).wait_send()
+
+    @pl.when(core == 0)
+    def _():
+        for b in order:
+            enter_right(b).wait_send()
+            enter_left(b).wait_send()
+
     for b in order:
-        for hop in range(HALF):
-            if hop + 1 < HALF or b < NB // 2:
-                send_right(b, hop).wait_send()
-            if hop + 1 < HALF or b >= NB // 2:
-                send_left(b, hop).wait_send()
         copy_y(b).wait_send()
 
 
@@ -498,12 +580,14 @@
             pltpu.VMEM((NB, MINE, BLK), BF),
             pltpu.VMEM((NB, MINE, BLK), F32),
             pltpu.VMEM((NB, BLK, HD), BF),
+            pltpu.VMEM((NB, NZ, BLK, HD), BF),
             dma((NK,)), dma((NK,)), dma, dma,
             dma((NB,)), dma((NB,)), dma((NB,)), dma((NB,)),
             dma((1,)), dma((1,)), dma((2, NB)), dma((2, NB)),
             dma((HALF,)), dma((HALF,)), dma((NX,)), dma((NX,)), dma((NX,)), dma((NX,)),
             dma((NB, HALF)), dma((NB, HALF)), dma((NB, NZ)), dma((NB,)), dma((NB,)),
             dma((2, NB)), dma((NB,)),
+            dma((NB, HALF)), dma((NB, HALF)), dma((NB, NZ)), dma((NB, NZ)),
         ],
         compiler_params=pltpu.CompilerParams(
             collective_id=0, has_side_effects=True, vmem_limit_bytes=60 * 1024 * 1024

time: 63.9 us -> 64.8 us (1.014)
  Pallas kernels: 61.6 us -> 62.6 us
    pallas_call x1, Pallas kernels: 61.6 us -> 62.6 us  [per_device(): pl.pallas_call(kernel, out_shape=jax.ShapeDtypeStruct((MINE, ROWS), BF),...]
where the time goes in v4:
time: 64.8 us; the launch traced here: 64.2 us
  Pallas kernels  62.6 us (97%)
  local copies, waits for them, and re-layouts  1.64 us (3%)
    pallas_call x1, Pallas kernels, per_device(): pl.pallas_call(kernel, out_shape=jax.ShapeDtypeStruct((MINE, ROWS), BF),...  62.6 us
    unnamed x1, local copies, waits for them, and re-layouts  1.64 us

profile of v4, /device:TPU:48, one launch (start us, length us, event | category | flops | bytes accessed | tf_op | source)
XLA Modules:
  0.0 64.2 jit_solution(6118586744218637518)
XLA Ops:
  0.0 62.6 %shard_map.64 = bf16[224,512]{1,0:T(8,128)(2,1)} custom-call(bf16[512,5376]{1,0:T(8,128)(2,1)} %x_hbm.1, f32[5376]{0:T(1024)} %gain_ref.1, bf16[5376,128]{1,0:T(8,128)(2,1)} %wq_hbm.1, bf16[5376,256]{1,0:T(8,128)(2,1)} %wkv_hbm.1, bf16[128,5376]{1,0:T(8,128)(2,1)} %wo_hbm.1, f32[1,128]{1,0:T(1,128)} %constant.2.clone.freq_ref), custom_call_target="tpu_custom_call" | custom-call | tf_op jit(solution)/shard_map/pallas_call | solution.py:559
  62.6 1.6 %copy.8 = bf16[224,512]{1,0:T(8,128)(2,1)} copy(bf16[224,512]{1,0:T(8,128)(2,1)} %shard_map.64) | data formatting | bytes 458752

commit v5 on v4

--- a/solution.py
+++ b/solution.py
@@ -293,11 +293,9 @@
     def spread():
         for j in range(HALF):
             copy_p1(j).wait_recv()
-        for dist in (2, 1, 3):
+        for dist in range(1, NX):
             copy_p2(dist).start()
         copy_sib(0, mine).start()
-
-    late = has_prev & (x == 0)
 
     @pl.when(passes)
     def _():
@@ -311,11 +309,6 @@
             copy_a(j).wait_recv()
             copy_b(j, yl).start()
             copy_c2(j, yl).start()
-
-        @pl.when(late)
-        def _():
-            spread()
-
         for j in order:
             copy_b(j, 1 - yl).wait_recv()
             copy_c2(j, 1 - yl).start()
@@ -325,11 +318,6 @@
         for j in order:
             copy_a(j).wait_recv()
             copy_b(j, yl).start()
-
-        @pl.when(late)
-        def _():
-            spread()
-
         for j in order:
             copy_c2(j, yl).wait_recv()
             copy_c2(j, 1 - yl).wait_recv()
@@ -347,6 +335,8 @@
         to = HALF if e == HALF - 1 else HALF + e + 1
         frm = 0 if e == 0 else HALF + e
         return copy(ho.at[b, frm], ho.at[b, to], l_s.at[b, e], g_r.at[b, to], s, left)
+
+    by_second = order[NB // 2 :]
 
     def send_right2(b, d):
         return copy(h2.at[b, d], h2.at[b, d + 1], r2_s.at[b, d], g2_r.at[b, d + 1], s, right)
@@ -402,23 +392,25 @@
         )
         ho[b, 0] = (mixed / total).astype(BF)
 
-        @pl.when(core == 1)
-        def _():
+        def first_hop():
             send_right(b, 0).start()
             send_left(b, 0).start()
 
-        @pl.when(core == 0)
-        def _():
-            enter_right(b).start()
-            enter_left(b).start()
-
-
-    @pl.when(jnp.logical_not(late))
-    def _():
-        spread()
-
-    def step(hop):
-        for b in order:
+        if b in by_second:
+            pl.when(core == 1)(first_hop)
+
+            @pl.when(core == 0)
+            def _():
+                enter_right(b).start()
+                enter_left(b).start()
+        else:
+            first_hop()
+
+
+    spread()
+
+    def step(hop, blocks):
+        for b in blocks:
             send_right(b, hop - 1).wait_recv()
             if goes_right(b, hop):
                 send_right(b, hop).start()
@@ -427,7 +419,7 @@
                 send_left(b, hop).start()
 
     def step2(hop):
-        for b in order:
+        for b in by_second:
             send_right2(b, hop - 1).wait_recv()
             if goes_right(b, hop):
                 send_right2(b, hop).start()
@@ -444,21 +436,24 @@
 
     @pl.when(core == 1)
     def _():
-        step(1)
+        step(1, order)
         for hop in range(1, HALF):
             if hop + 1 < HALF:
-                step(hop + 1)
+                step(hop + 1, order)
             step2(hop)
-            if hop == HALF - 2:
+            if hop == 3:
                 spread_on()
-        for b in order:
+        for b in by_second:
             send_right2(b, HALF - 1).wait_recv()
             hand(b, HALF).start()
 
     @pl.when(core == 0)
     def _():
-        spread_on()
-        for b in order:
+        for hop in range(1, HALF):
+            step(hop, order[: NB // 2])
+            if hop == 3:
+                spread_on()
+        for b in by_second:
             for i in range(1, NZ):
                 if i != HALF:
                     hand(b, i).wait_recv()
@@ -525,24 +520,31 @@
         copy_p2(dist).wait_send()
     for dist in range(NX):
         copy_sib(dist, mine).wait_send()
-    @pl.when(core == 1)
-    def _():
-        for b in order:
+    def ring_left(blocks):
+        for b in blocks:
             for hop in range(HALF):
                 if goes_right(b, hop):
                     send_right(b, hop).wait_send()
-                    if hop > 0:
-                        send_right2(b, hop).wait_send()
                 if goes_left(b, hop):
                     send_left(b, hop).wait_send()
-                    if hop > 0:
-                        send_left2(b, hop).wait_send()
+
+    ring_left(order[: NB // 2])
+
+    @pl.when(core == 1)
+    def _():
+        ring_left(by_second)
+        for b in by_second:
+            for hop in range(1, HALF):
+                if goes_right(b, hop):
+                    send_right2(b, hop).wait_send()
+                if goes_left(b, hop):
+                    send_left2(b, hop).wait_send()
             for i in range(1, NZ):
                 hand(b, i).wait_send()
 
     @pl.when(core == 0)
     def _():
-        for b in order:
+        for b in by_second:
             enter_right(b).wait_send()
             enter_left(b).wait_send()
 

time: 64.8 us -> 64.9 us (level)
  no operation moved by 1% of the time
where the time goes in v5:
time: 64.9 us; the launch traced here: 64.3 us
  Pallas kernels  62.6 us (96%)
  local copies, waits for them, and re-layouts  1.64 us (3%)
    pallas_call x1, Pallas kernels, per_device(): pl.pallas_call(kernel, out_shape=jax.ShapeDtypeStruct((MINE, ROWS), BF),...  62.6 us
    unnamed x1, local copies, waits for them, and re-layouts  1.64 us

profile of v5, /device:TPU:48, one launch (start us, length us, event | category | flops | bytes accessed | tf_op | source)
XLA Modules:
  0.0 64.3 jit_solution(9263723519439104851)
XLA Ops:
  0.0 62.6 %shard_map.64 = bf16[224,512]{1,0:T(8,128)(2,1)} custom-call(bf16[512,5376]{1,0:T(8,128)(2,1)} %x_hbm.1, f32[5376]{0:T(1024)} %gain_ref.1, bf16[5376,128]{1,0:T(8,128)(2,1)} %wq_hbm.1, bf16[5376,256]{1,0:T(8,128)(2,1)} %wkv_hbm.1, bf16[128,5376]{1,0:T(8,128)(2,1)} %wo_hbm.1, f32[1,128]{1,0:T(1,128)} %constant.2.clone.freq_ref), custom_call_target="tpu_custom_call" | custom-call | tf_op jit(solution)/shard_map/pallas_call | solution.py:561
  62.6 1.6 %copy.8 = bf16[224,512]{1,0:T(8,128)(2,1)} copy(bf16[224,512]{1,0:T(8,128)(2,1)} %shard_map.64) | data formatting | bytes 458752

commit v6 on v2

--- a/solution.py
+++ b/solution.py
@@ -306,9 +306,14 @@
         return copy(ho.at[b, d], ho.at[b, d + 1], r_s.at[b, d], g_r.at[b, d + 1], s, right)
 
     def send_left(b, e):
-        to = HALF if e == HALF - 1 else HALF + e + 1
         frm = 0 if e == 0 else HALF + e
+        to = HALF + e + 1
         return copy(ho.at[b, frm], ho.at[b, to], l_s.at[b, e], g_r.at[b, to], s, left)
+
+    def send_last(b):
+        frm, to = (HALF - 2, at_z(2)) if b < NB // 2 else (NZ - 2, at_z(-2))
+        sem = (r_s if b < NB // 2 else l_s).at[b, HALF - 1]
+        return copy(ho.at[b, frm], ho.at[b, HALF], sem, g_r.at[b, HALF], s, to)
 
     first_key = jnp.maximum(WINDOW - ROWS * s, 0)
     query_row = lax.broadcasted_iota(jnp.int32, (BLK, BLK), 0)
@@ -369,10 +374,14 @@
     for hop in range(1, HALF):
         for b in order:
             send_right(b, hop - 1).wait_recv()
-            if hop + 1 < HALF or b < NB // 2:
+            if hop + 2 == HALF and b < NB // 2:
+                send_last(b).start()
+            if hop + 1 < HALF:
                 send_right(b, hop).start()
             send_left(b, hop - 1).wait_recv()
-            if hop + 1 < HALF or b >= NB // 2:
+            if hop + 2 == HALF and b >= NB // 2:
+                send_last(b).start()
+            if hop + 1 < HALF:
                 send_left(b, hop).start()
         if hop == 3:
             for dist in range(1, NX):
@@ -396,10 +405,7 @@
     for b in order:
         theirs = product(b, early, theirs_at)
         mine_part = product(b, early, mine_at)
-        if b < NB // 2:
-            send_right(b, HALF - 1).wait_recv()
-        else:
-            send_left(b, HALF - 1).wait_recv()
+        send_last(b).wait_recv()
         psend[b] = (theirs + product(b, [HALF], theirs_at)).astype(BF)
         copy_y(b).start()
         own[b] = mine_part + product(b, [HALF], mine_at)
@@ -444,11 +450,10 @@
     for dist in range(NX):
         copy_sib(dist, mine).wait_send()
     for b in order:
-        for hop in range(HALF):
-            if hop + 1 < HALF or b < NB // 2:
-                send_right(b, hop).wait_send()
-            if hop + 1 < HALF or b >= NB // 2:
-                send_left(b, hop).wait_send()
+        for hop in range(HALF - 1):
+            send_right(b, hop).wait_send()
+            send_left(b, hop).wait_send()
+        send_last(b).wait_send()
         copy_y(b).wait_send()
 
 

time: 62.6 us -> 63.4 us (1.013)
  the two profiles are of different devices: /device:TPU:48 before, /device:TPU:32 now
where the time goes in v6:
time: 63.4 us; the launch traced here: 63.2 us
  Pallas kernels  61.5 us (97%)
  local copies, waits for them, and re-layouts  1.64 us (3%)
    pallas_call x1, Pallas kernels, per_device(): pl.pallas_call(kernel, out_shape=jax.ShapeDtypeStruct((MINE, ROWS), BF),...  61.5 us
    unnamed x1, local copies, waits for them, and re-layouts  1.64 us

profile of v6, /device:TPU:32, one launch (start us, length us, event | category | flops | bytes accessed | tf_op | source)
XLA Modules:
  0.0 63.2 jit_solution(4541071739824295833)
XLA Ops:
  0.0 61.5 %shard_map.64 = bf16[224,512]{1,0:T(8,128)(2,1)} custom-call(bf16[512,5376]{1,0:T(8,128)(2,1)} %x_hbm.1, f32[5376]{0:T(1024)} %gain_ref.1, bf16[5376,128]{1,0:T(8,128)(2,1)} %wq_hbm.1, bf16[5376,256]{1,0:T(8,128)(2,1)} %wkv_hbm.1, bf16[128,5376]{1,0:T(8,128)(2,1)} %wo_hbm.1, f32[1,128]{1,0:T(1,128)} %constant.2.clone.freq_ref), custom_call_target="tpu_custom_call" | custom-call | tf_op jit(solution)/shard_map/pallas_call | solution.py:466
  61.5 1.6 %copy.8 = bf16[224,512]{1,0:T(8,128)(2,1)} copy(bf16[224,512]{1,0:T(8,128)(2,1)} %shard_map.64) | data formatting | bytes 458752
